TPU v7x, 32 devices: a whole 2x2x4 slice. The times are simulated.
32 devices in a mesh: cen: 8 (over y, x, core), grp: 4 (over z).
Axes of the slice: x: 2, y: 2, z: 4, core: 2. Of those that a mesh axis runs over, the one named last changes fastest.
Arguments:
- centers: bfloat16 [65536, 1024], P(('cen', 'grp')), may hold values from -2 to 2
- coefficients: float32 [65536, 256], P(('cen', 'grp')), may hold values from -0.09375 to 0.09375
- batch_index: int32 [256], P(('cen', 'grp')), may hold values from 0 to 65535, as said below
- batch_labels: float32 [256, 256], P(('cen', 'grp')), may hold values from -24 to 24
- nystrom_index: int32 [16384], P(('cen', 'grp')), may hold values from 0 to 65535, as said below
- eigenvectors: float32 [16384, 512], P(('cen', 'grp')), may hold values from -0.046875 to 0.046875
- eigen_weights: float32 [512], replicated, may hold values from 0.002 to 0.05
Outputs:
- residual: float32 [256, 256], P(('cen', 'grp'))
- correction: float32 [16384, 256], P(('cen', 'grp'))
Inputs may be any that keep to these rules, and one draw needn't show every extreme that they name: `batch_index`: for each j, entries 8 * j to 8 * j + 7 are distinct rows among j * 2048 to j * 2048 + 2047. `nystrom_index`: for each j, entries 512 * j to 512 * j + 511 are distinct rows among j * 2048 to j * 2048 + 2047.
All inputs are finite; a program needn't handle non-finite values.
Results may differ from a plain program's by a relative error of at most 0.0003.
Values may be sent and summed in bfloat16 or wider, within the bound.
No kernel may reach another device: no remote copies, remote signals or barrier semaphores. Data moves between devices by JAX's collectives and lax.ppermute only.
A program may use at most 64 MiB of HBM per device.

v0:
```python
import jax
import jax.numpy as jnp
from jax import lax
from jax.sharding import PartitionSpec as P


def inner_kernel(left, right):
    scores = lax.dot_general(
        left, right, (((1,), (1,)), ((), ())), preferred_element_type=jnp.float32
    )
    return jnp.exp(scores / 32.0)


def exact_dot(left, right):
    return jnp.dot(left, right, precision=lax.Precision.HIGHEST, preferred_element_type=jnp.float32)


def body(
    centers, coefficients, batch_index, batch_labels, nystrom_index, eigenvectors, eigen_weights
):
    center_count = centers.shape[0]
    owned_rows = jnp.take(centers, batch_index % center_count, axis=0)
    batch_x = lax.all_gather(owned_rows, ("cen", "grp"), axis=0, tiled=True)
    partial_pred = exact_dot(inner_kernel(batch_x, centers), coefficients)
    nystrom_x = jnp.take(centers, nystrom_index % center_count, axis=0)
    nystrom_kernel = inner_kernel(nystrom_x, batch_x)
    batch_rows = batch_labels.shape[0]
    first_row = lax.axis_index(("cen", "grp")) * batch_rows
    own_part = lax.dynamic_slice_in_dim(partial_pred, first_row, batch_rows, 0) - batch_labels
    summand = lax.dynamic_update_slice_in_dim(partial_pred, own_part, first_row, 0)
    residual_all = lax.psum(summand, ("cen", "grp"))
    own_residual = lax.dynamic_slice_in_dim(residual_all, first_row, batch_rows, 0)
    local_products = exact_dot(nystrom_kernel, residual_all)
    projected = lax.psum(exact_dot(eigenvectors.T, local_products), ("cen", "grp"))
    correction = exact_dot(eigenvectors, eigen_weights[:, None] * projected)
    return (own_residual, correction)


def solution(mesh):
    in_specs = (
        P(("cen", "grp"), None),
        P(("cen", "grp"), None),
        P(("cen", "grp")),
        P(("cen", "grp"), None),
        P(("cen", "grp")),
        P(("cen", "grp"), None),
        P(),
    )
    out_specs = (P(("cen", "grp"), None), P(("cen", "grp"), None))
    return jax.shard_map(body, mesh=mesh, in_specs=in_specs, out_specs=out_specs, check_vma=False)
```

profile of v0, /device:TPU:0, one launch (start us, length us, event | category | flops | bytes accessed | tf_op | source)
XLA Modules:
  0.0 365.1 jit_solution(11219667917849283521)
XLA Ops:
  7.2 0.0 copy-start
  7.2 0.0 all-reduce.3.cloned.1.call-start
  7.2 0.8 compare_and_fusion.1
  8.0 3.3 gather_fusion
  11.4 0.1 broadcast_select_fusion
  11.4 73.9 %all_gather.3 = bf16[256,1024]{1,0:T(8,128)(2,1)S(1)} all-gather(bf16[8,1024]{1,0:T(8,128)(2,1)S(1)} %broadcast_select_fusion), channel_id=1, replica_groups=mesh['cen'=8,'grp'=4] {'cen','grp'}, dimensions={0}, use_global_device_ids=true | all-gather | bytes 540672 | tf_op jit(solution)/shard_map/all_gather | solution.py:23
  85.4 0.0 copy-start.3
  85.4 0.8 copy-done.3
  86.2 4.9 %fusion = f32[256,2048]{1,0:T(8,128)} fusion(bf16[256,1024]{1,0:T(8,128)(2,1)S(1)} %all_gather.3, bf16[2048,1024]{1,0:T(8,128)(2,1)} %param.7), kind=kOutput, calls=%fused_computation.3 | convolution fusion | flops 1074266112 | bytes 6815744 | tf_op jit(solution)/shard_map/dot_general | solution.py:8
  91.1 0.0 copy-done
  91.1 0.0 copy-start.4
  91.1 0.0 copy-start.6
  91.1 3.5 fusion.10
  94.6 0.0 copy-done.4
  94.6 0.0 copy-start.2
  94.6 0.7 copy-done.2
  95.3 0.0 all-reduce.3.cloned.1.call-update
  95.4 0.0 all-reduce.5.cloned.1.call-start
  95.4 0.0 copy-done.6
  95.5 6.2 %gather_fusion.1 = bf16[512,1024]{1,0:T(8,128)(2,1)} fusion(bf16[2048,1024]{1,0:T(8,128)(2,1)} %param.7, s32[1024]{0:T(1024)S(1)} %pad_clamp_fusion), kind=kCustom, calls=%fused_computation.1 | custom fusion | bytes 2099200 | tf_op jit(solution)/shard_map/jit(_take)/gather | solution.py:25
  101.7 0.0 copy-start.1
  101.7 2.8 fusion.1
  104.4 0.0 copy-start.5
  104.4 114.0 %all-reduce.3.cloned.1.call-done = f32[256,256]{1,0:T(8,128)} async-done(((f32[256,256]{1,0:T(8,128)}), f32[256,256]{1,0:T(8,128)}) %all-reduce.3.cloned.1.call-update) | async-done | bytes 262160 | tf_op jit(solution)/shard_map/psum | solution.py:31
  218.5 1.7 fusion.11
  220.2 0.0 copy-done.1
  220.2 2.6 convolution_bitcast_fusion.1
  222.8 0.0 all-reduce.5.cloned.1.call-update
  222.8 1.3 constant_dynamic-slice_fusion
  224.1 128.4 %all-reduce.5.cloned.1.call-done = f32[512,256]{1,0:T(8,128)} async-done(((f32[512,256]{1,0:T(8,128)}), f32[512,256]{1,0:T(8,128)}) %all-reduce.5.cloned.1.call-update) | async-done | bytes 524304 | tf_op jit(solution)/shard_map/psum | solution.py:34
  352.5 0.0 copy-done.5
  352.5 3.8 %convolution_bitcast_fusion = f32[512,256]{0,1:T(8,128)} fusion(f32[512,512]{1,0:T(8,128)S(1)} %copy-done.1, f32[512,256]{1,0:T(8,128)} %all-reduce.5.cloned.1.call-done, f32[512]{0:T(512)S(1)} %copy-done.5), kind=kOutput, calls=%fused_computation.6 | convolution fusion | flops 805437440 | bytes 2099200 | tf_op jit(solution)/shard_map/dot_general | solution.py:15
  356.2 2.0 copy.9
  (4 shorter events, 0.0 us)
Async XLA Ops:
  7.2 83.9 %copy-start = (f32[2048,256]{1,0:T(8,128)S(1)}, f32[2048,256]{1,0:T(8,128)}, u32[]{:S(2)}) copy-start(f32[2048,256]{1,0:T(8,128)} %param.8) | copy-start | bytes 6291460
  7.2 211.3 %all-reduce.3.cloned.1.call-start = ((), (), s32[]{:S(2)}) async-start(), calls=%async_computation | async-start | bytes 524288 | tf_op jit(solution)/shard_map/psum | solution.py:31
  85.4 0.8 copy-start.3
  91.1 3.5 copy-start.4
  91.1 4.3 %copy-start.6 = (s32[512]{0:T(512)S(1)}, s32[512]{0:T(512)}, u32[]{:S(2)}) copy-start(s32[512]{0:T(512)} %param.11) | copy-start | bytes 6148
  94.6 0.7 copy-start.2
  95.4 257.1 %all-reduce.5.cloned.1.call-start = ((), (), s32[]{:S(2)}) async-start(), calls=%async_computation.1 | async-start | bytes 1048576 | tf_op jit(solution)/shard_map/psum | solution.py:34
  101.7 118.5 %copy-start.1 = (f32[512,512]{1,0:T(8,128)S(1)}, f32[512,512]{1,0:T(8,128)}, u32[]{:S(2)}) copy-start(f32[512,512]{1,0:T(8,128)} %param.12) | copy-start | bytes 3145732
  104.4 248.0 %copy-start.5 = (f32[512]{0:T(512)S(1)}, f32[512]{0:T(512)}, u32[]{:S(2)}) copy-start(f32[512]{0:T(512)} %param.13) | copy-start | bytes 6148
Sparse Core Ops, SparseCore 0:
  95.5 122.9 all-reduce.2
  224.3 128.1 all-reduce.4
where the time goes:
time: 366 us; the launch traced here: 365 us
  waiting for transfers between devices  242 us (66%)
  blocking collectives  73.9 us (20%)
  matrix products  19.3 us (5%)
  local copies, waits for them, and re-layouts  14.4 us (4%)
  between operations  14.1 us (4%)
    psum x1, waiting for transfers between devices, body(): lax.psum(exact_dot(eigenvectors.T, local_products), ('cen', 'grp'))  128 us
    psum x1, waiting for transfers between devices, body(): residual_all = lax.psum(summand, ('cen', 'grp'))  114 us
    all_gather x1, blocking collectives, body(): batch_x = lax.all_gather(owned_rows, ('cen', 'grp'), axis=0, tiled=True)  73.9 us
    dot_general x4, matrix products, exact_dot(): jnp.dot(left, right, precision=lax.Precision.HIGHEST, preferred_element_t...  11.6 us
    dot_general x2, matrix products, inner_kernel(): lax.dot_general(left, right, (((1,), (1,)), ((), ())), preferred_element_...  7.7 us
  transfers between devices with their start and end apart: 2, of which 2 were waited for; matrix products, arithmetic and copies ran while one was open for 3% of the time, Pallas kernels for 0%

commit v1 on v0

--- a/solution.py
+++ b/solution.py
@@ -31,7 +31,7 @@
     residual_all = lax.psum(summand, ("cen", "grp"))
     own_residual = lax.dynamic_slice_in_dim(residual_all, first_row, batch_rows, 0)
     local_products = exact_dot(nystrom_kernel, residual_all)
-    projected = lax.psum(exact_dot(eigenvectors.T, local_products), ("cen", "grp"))
+    projected = lax.psum(lax.psum(exact_dot(eigenvectors.T, local_products), "grp"), "cen")
     correction = exact_dot(eigenvectors, eigen_weights[:, None] * projected)
     return (own_residual, correction)
 

time: 366 us -> 331 us (0.904)
  waiting for transfers between devices: 242 us -> 208 us
    psum x1 -> x2, waiting for transfers between devices: 128 us -> 94.1 us  [the longest x1 56.4 us: body(): lax.psum(lax.psum(exact_dot(eigenvectors.T, local_products), 'grp'), 'cen')]
  transfers between devices with their start and end apart: 2 -> 3, of which waited for: 2 -> 3; matrix products, arithmetic and copies ran while one was open for 3% -> 3% of each run, Pallas kernels for 0% -> 0%
where the time goes in v1:
time: 331 us
  waiting for transfers between devices  208 us (63%)
  blocking collectives  73.9 us (22%)
  matrix products  19.3 us (6%)
  local copies, waits for them, and re-layouts  14.4 us (4%)
  between operations  13.8 us (4%)
    psum x1, waiting for transfers between devices, body(): residual_all = lax.psum(summand, ('cen', 'grp'))  114 us
    all_gather x1, blocking collectives, body(): batch_x = lax.all_gather(owned_rows, ('cen', 'grp'), axis=0, tiled=True)  73.9 us
    psum x1, waiting for transfers between devices, body(): lax.psum(lax.psum(exact_dot(eigenvectors.T, local_products), 'grp'), 'cen')  56.4 us
    psum x1, waiting for transfers between devices, body(): lax.psum(exact_dot(eigenvectors.T, local_products), 'grp')  37.7 us
    dot_general x4, matrix products, exact_dot(): jnp.dot(left, right, precision=lax.Precision.HIGHEST, preferred_element_t...  11.6 us
    dot_general x2, matrix products, inner_kernel(): lax.dot_general(left, right, (((1,), (1,)), ((), ())), preferred_element_...  7.7 us
  transfers between devices with their start and end apart: 3, of which 3 were waited for; matrix products, arithmetic and copies ran while one was open for 3% of the time, Pallas kernels for 0%

profile of v1, /device:TPU:0, one launch (start us, length us, event | category | flops | bytes accessed | tf_op | source)
XLA Modules:
  0.0 330.6 jit_solution(1303284142650349051)
XLA Ops:
  7.2 0.0 copy-start
  7.2 0.0 all-reduce.4.cloned.1.call-start
  7.2 0.8 compare_and_fusion.1
  8.0 3.3 %gather_fusion = bf16[8,1024]{1,0:T(8,128)(2,1)S(1)} fusion(bf16[2048,1024]{1,0:T(8,128)(2,1)} %param.7, s32[1024]{0:T(1024)S(1)} %pad_clamp_fusion.1), kind=kCustom, calls=%fused_computation | custom fusion | bytes 32800 | tf_op jit(solution)/shard_map/jit(_take)/gather | solution.py:22
  11.4 0.1 broadcast_select_fusion
  11.4 73.9 %all_gather.3 = bf16[256,1024]{1,0:T(8,128)(2,1)S(1)} all-gather(bf16[8,1024]{1,0:T(8,128)(2,1)S(1)} %broadcast_select_fusion), channel_id=1, replica_groups=mesh['cen'=8,'grp'=4] {'cen','grp'}, dimensions={0}, use_global_device_ids=true | all-gather | bytes 540672 | tf_op jit(solution)/shard_map/all_gather | solution.py:23
  85.4 0.0 copy-start.3
  85.4 0.8 copy-done.3
  86.2 4.9 %fusion = f32[256,2048]{1,0:T(8,128)} fusion(bf16[256,1024]{1,0:T(8,128)(2,1)S(1)} %all_gather.3, bf16[2048,1024]{1,0:T(8,128)(2,1)} %param.7), kind=kOutput, calls=%fused_computation.3 | convolution fusion | flops 1074266112 | bytes 6815744 | tf_op jit(solution)/shard_map/dot_general | solution.py:8
  91.1 0.0 copy-done
  91.1 0.0 copy-start.4
  91.1 0.0 copy-start.6
  91.1 3.5 %fusion.10 = f32[256,256]{1,0:T(8,128)S(1)} fusion(f32[256,2048]{1,0:T(8,128)} %fusion, f32[2048,256]{1,0:T(8,128)S(1)} %copy-done), kind=kOutput, calls=%fused_computation.31 | convolution fusion | flops 1610612736 | bytes 4456448 | tf_op jit(solution)/shard_map/dot_general | solution.py:15
  94.6 0.0 copy-done.4
  94.6 0.0 copy-start.2
  94.6 0.7 copy-done.2
  95.3 0.0 all-reduce.4.cloned.1.call-update
  95.4 0.0 all-reduce.6.cloned.1.call-start
  95.4 0.0 copy-done.6
  95.5 6.2 %gather_fusion.1 = bf16[512,1024]{1,0:T(8,128)(2,1)} fusion(bf16[2048,1024]{1,0:T(8,128)(2,1)} %param.7, s32[1024]{0:T(1024)S(1)} %pad_clamp_fusion), kind=kCustom, calls=%fused_computation.1 | custom fusion | bytes 2099200 | tf_op jit(solution)/shard_map/jit(_take)/gather | solution.py:25
  101.7 0.0 copy-start.1
  101.7 2.8 fusion.1
  104.4 0.0 copy-start.5
  104.4 114.0 %all-reduce.4.cloned.1.call-done = f32[256,256]{1,0:T(8,128)} async-done(((f32[256,256]{1,0:T(8,128)}), f32[256,256]{1,0:T(8,128)}) %all-reduce.4.cloned.1.call-update) | async-done | bytes 262160 | tf_op jit(solution)/shard_map/psum | solution.py:31
  218.5 1.7 fusion.11
  220.2 0.0 copy-done.1
  220.2 2.6 convolution_bitcast_fusion.1
  222.8 0.0 all-reduce.6.cloned.1.call-update
  222.8 0.0 all-reduce.8.cloned.1.call-start
  222.9 37.7 %all-reduce.6.cloned.1.call-done = f32[512,256]{1,0:T(8,128)} async-done(((f32[512,256]{1,0:T(8,128)}), f32[512,256]{1,0:T(8,128)}) %all-reduce.6.cloned.1.call-update) | async-done | bytes 524304 | tf_op jit(solution)/shard_map/psum | solution.py:34
  260.5 0.0 all-reduce.8.cloned.1.call-update
  260.5 1.3 constant_dynamic-slice_fusion
  261.9 56.4 %all-reduce.8.cloned.1.call-done = f32[512,256]{1,0:T(8,128)} async-done(((f32[512,256]{1,0:T(8,128)}), f32[512,256]{1,0:T(8,128)}) %all-reduce.8.cloned.1.call-update) | async-done | bytes 524304 | tf_op jit(solution)/shard_map/psum | solution.py:34
  318.3 0.0 copy-done.5
  318.3 3.8 %convolution_bitcast_fusion = f32[512,256]{0,1:T(8,128)} fusion(f32[512,512]{1,0:T(8,128)S(1)} %copy-done.1, f32[512,256]{1,0:T(8,128)} %all-reduce.8.cloned.1.call-done, f32[512]{0:T(512)S(1)} %copy-done.5), kind=kOutput, calls=%fused_computation.6 | convolution fusion | flops 805437440 | bytes 2099200 | tf_op jit(solution)/shard_map/dot_general | solution.py:15
  322.1 2.0 copy.9
  (4 shorter events, 0.0 us)
Async XLA Ops:
  7.2 83.9 %copy-start = (f32[2048,256]{1,0:T(8,128)S(1)}, f32[2048,256]{1,0:T(8,128)}, u32[]{:S(2)}) copy-start(f32[2048,256]{1,0:T(8,128)} %param.8) | copy-start | bytes 6291460
  7.2 211.3 %all-reduce.4.cloned.1.call-start = ((), (), s32[]{:S(2)}) async-start(), calls=%async_computation | async-start | bytes 524288 | tf_op jit(solution)/shard_map/psum | solution.py:31
  85.4 0.8 copy-start.3
  91.1 3.5 %copy-start.4 = (f32[8,256]{1,0:T(8,128)S(1)}, f32[8,256]{1,0:T(8,128)}, u32[]{:S(2)}) copy-start(f32[8,256]{1,0:T(8,128)} %param.10) | copy-start | bytes 24580
  91.1 4.3 %copy-start.6 = (s32[512]{0:T(512)S(1)}, s32[512]{0:T(512)}, u32[]{:S(2)}) copy-start(s32[512]{0:T(512)} %param.11) | copy-start | bytes 6148
  94.6 0.7 copy-start.2
  95.4 165.2 %all-reduce.6.cloned.1.call-start = ((), (), s32[]{:S(2)}) async-start(), calls=%async_computation.1 | async-start | bytes 1048576 | tf_op jit(solution)/shard_map/psum | solution.py:34
  101.7 118.5 %copy-start.1 = (f32[512,512]{1,0:T(8,128)S(1)}, f32[512,512]{1,0:T(8,128)}, u32[]{:S(2)}) copy-start(f32[512,512]{1,0:T(8,128)} %param.12) | copy-start | bytes 3145732
  104.4 213.9 %copy-start.5 = (f32[512]{0:T(512)S(1)}, f32[512]{0:T(512)}, u32[]{:S(2)}) copy-start(f32[512]{0:T(512)} %param.13) | copy-start | bytes 6148
  222.8 95.5 %all-reduce.8.cloned.1.call-start = ((), (), s32[]{:S(2)}) async-start(), calls=%async_computation.2 | async-start | bytes 1048576 | tf_op jit(solution)/shard_map/psum | solution.py:34
Sparse Core Ops, SparseCore 0:
  95.5 122.9 all-reduce.3
  222.9 37.5 all-reduce.5
  263.6 54.6 all-reduce.7
